TPU v7x, 512 devices: a whole 4x4x16 slice. The times are simulated.
512 devices in a mesh: gx: 32 (over z, x_lo), gy: 16 (over x_hi, y, core).
Axes of the slice: x: 4 (x_hi: 2, x_lo: 2; x = x_hi * 2 + x_lo), y: 4, z: 16, core: 2. Of those that a mesh axis runs over, the one named last changes fastest.
Arguments:
- adjoint_forcing: float32 [4, 6, 1024, 4096], P(None, None, 'gx', 'gy'), may hold values from -6 to 6
- field_mixing: float32 [4, 4], replicated, may hold values from -3 to 3
- time_mixing: float32 [6, 6], replicated, may hold values from -2.5 to 2.5
- kernel_east: float32 [21], replicated, may hold values from 0.1 to 1
- kernel_north: float32 [21], replicated, may hold values from 0.1 to 1
- spatial_modes: bfloat16 [1024, 4096, 256], P('gx', 'gy'), may hold values from -0.00390625 to 0.00390625
- coefficients: float32 [256, 24], P('gy'), may hold values from -6 to 6
Outputs:
- gradient: float32 [256, 24], P('gy')
All inputs are finite; a program needn't handle non-finite values.
Results may differ from a plain program's by a relative error of at most 0.0029.
Values sent between devices are 32-bit elements; how exact they have to be, the bound alone decides.
A program may use at most 64 MiB of HBM per device.

v0:
```python
import jax
import jax.numpy as jnp
from jax import lax
from jax.sharding import PartitionSpec as P


def padded(block, sides, width):
    for axis, dim in sides:
        count = lax.axis_size(axis)
        forward = [(i, i + 1) for i in range(count - 1)]
        backward = [(target, source) for source, target in forward]
        low = lax.ppermute(
            lax.slice_in_dim(block, block.shape[dim] - width, None, axis=dim), axis, forward
        )
        high = lax.ppermute(lax.slice_in_dim(block, 0, width, axis=dim), axis, backward)
        block = jnp.concatenate([low, block, high], axis=dim)
    return block


def smooth_valid(extended, taps, axis, count):
    total = taps[0] * lax.slice_in_dim(extended, 0, count, axis=axis)
    for j in range(1, taps.shape[0]):
        total = total + taps[j] * lax.slice_in_dim(extended, j, j + count, axis=axis)
    return total


def local(
    adjoint_forcing,
    field_mixing,
    time_mixing,
    kernel_east,
    kernel_north,
    spatial_modes,
    coefficients,
):
    fields, levels, width_x, width_y = adjoint_forcing.shape
    reach = (kernel_east.shape[0] - 1) // 2
    mixed = jnp.einsum(
        "gf,st,gsxy->ftxy",
        field_mixing,
        time_mixing,
        adjoint_forcing,
        precision=lax.Precision.HIGHEST,
    )
    wide_x = padded(mixed, (("gx", 2),), reach)
    along_x = smooth_valid(wide_x, kernel_east, 2, width_x)
    wide_y = padded(along_x, (("gy", 3),), reach)
    smoothed = smooth_valid(wide_y, kernel_north, 3, width_y)
    smoothed = smoothed.astype(jnp.bfloat16)
    flat_state = smoothed.reshape(fields * levels, width_x * width_y)
    flat_modes = spatial_modes.reshape(width_x * width_y, spatial_modes.shape[2])
    projection = lax.dot_general(
        flat_modes, flat_state, (((0,), (1,)), ((), ())), preferred_element_type=jnp.float32
    )
    owned = coefficients.shape[0]
    total = lax.psum(projection, ("gx", "gy"))
    mine = lax.dynamic_slice_in_dim(total, lax.axis_index("gy") * owned, owned, 0)
    return coefficients + mine


def solution(mesh):
    in_specs = (P(None, None, "gx", "gy"), P(), P(), P(), P(), P("gx", "gy", None), P("gy", None))
    out_specs = P("gy", None)
    return jax.shard_map(local, mesh=mesh, in_specs=in_specs, out_specs=out_specs, check_vma=False)
```

profile of v0, /device:TPU:1, one launch (start us, length us, event | category | flops | bytes accessed | tf_op | source)
XLA Modules:
  0.0 193.7 jit_solution(18179628404483678090)
XLA Ops:
  0.0 0.0 copy-start
  0.0 3.1 %fusion.118 = f32[6,32,256,4]{2,3,1,0:T(4,128)S(1)} fusion(f32[4,6,32,256]{3,2,1,0:T(8,128)} %param.7, f32[4,4]{1,0:T(4,128)} %param.8), kind=kOutput, calls=%fused_computation.196 | convolution fusion | flops 9437184 | bytes 1572928 | tf_op jit(solution)/shard_map/gf,st,gsxy->ftxy/dot_general | solution.py:38
  3.1 0.0 copy-done
  3.1 0.0 copy-start.2
  3.1 0.0 copy-start.3
  3.1 1.5 convolution_bitcast_fusion
  4.6 0.1 fusion.123
  4.6 4.0 %collective-permute-start = (f32[4,6,10,256]{3,1,0,2:T(8,128)S(1)}, f32[4,6,10,256]{3,1,0,2:T(8,128)S(1)}, u32[]{:S(2)}, u32[]{:S(2)}) collective-permute-start(f32[4,6,10,256]{3,1,0,2:T(8,128)S(1)} %get-tuple-element.7), channel_id=1, source_target_pairs={{0,16},{16,32},{32,48},{48,64},{64,80},{80,96},{96,112},{112,128},... | collective-permute-start | bytes 737288 | tf_op jit(solution)/shard_map/ppermute | solution.py:12
  8.6 1.3 collective-permute-start.1
  9.9 0.0 copy-done.2
  9.9 0.7 fusion.127
  10.6 0.7 fusion.126
  11.3 0.0 copy-done.3
  11.3 0.7 fusion.124
  12.0 0.6 collective-permute-done
  12.6 4.0 %collective-permute-done.1 = f32[4,6,10,256]{3,1,0,2:T(8,128)S(1)} collective-permute-done((f32[4,6,10,256]{3,1,0,2:T(8,128)S(1)}, f32[4,6,10,256]{3,1,0,2:T(8,128)S(1)}, u32[]{:S(2)}, u32[]{:S(2)}) %collective-permute-start.1) | collective-permute-done | bytes 245792 | tf_op jit(solution)/shard_map/ppermute | solution.py:15
  16.5 15.8 %fusion.3 = f32[4,6,32,256]{3,1,0,2:T(8,128)S(1)} fusion(f32[4,6,32,256]{3,1,0,2:T(8,128)S(1)} %convolution_bitcast_fusion, f32[4,6,10,256]{3,1,0,2:T(8,128)S(1)} %collective-permute-done.1, f32[4,6,10,256]{3,1,0,2:T(8,128)S(1)} %collective-permute-done, f32[]{:T(128)} %bitcast.24, f32[]{:T(128)} %bitcast.23, f32[]{:T(128)} %bitcast.22, f32[]{:T(128)} %bitcast.21, ...), kind=kLoop, calls=%fused_computation.77 | loop fusion | flops 11993088 | bytes 2064468 | tf_op jit(solution)/shard_map/add | solution.py:23
  32.4 0.2 fusion.122
  32.6 10.0 %collective-permute-start.2 = (f32[4,6,32,10]{3,1,0,2:T(8,128)S(1)}, f32[4,6,32,10]{3,1,0,2:T(8,128)S(1)}, u32[]{:S(2)}, u32[]{:S(2)}) collective-permute-start(f32[4,6,32,10]{3,1,0,2:T(8,128)S(1)} %get-tuple-element.5), channel_id=1, source_target_pairs={{0,1},{1,2},{2,3},{3,4},{4,5},{5,6},{6,7},{7,8},{8,9},{9,10},{10,1... | collective-permute-start | bytes 92168 | tf_op jit(solution)/shard_map/ppermute | solution.py:12
  42.6 1.9 collective-permute-start.3
  44.6 0.7 fusion.125
  45.2 3.5 %collective-permute-done.2 = f32[4,6,32,10]{3,1,0,2:T(8,128)S(1)} collective-permute-done((f32[4,6,32,10]{3,1,0,2:T(8,128)S(1)}, f32[4,6,32,10]{3,1,0,2:T(8,128)S(1)}, u32[]{:S(2)}, u32[]{:S(2)}) %collective-permute-start.2) | collective-permute-done | bytes 30752 | tf_op jit(solution)/shard_map/ppermute | solution.py:12
  48.7 4.4 %collective-permute-done.3 = f32[4,6,32,10]{3,1,0,2:T(8,128)S(1)} collective-permute-done((f32[4,6,32,10]{3,1,0,2:T(8,128)S(1)}, f32[4,6,32,10]{3,1,0,2:T(8,128)S(1)}, u32[]{:S(2)}, u32[]{:S(2)}) %collective-permute-start.3) | collective-permute-done | bytes 30752 | tf_op jit(solution)/shard_map/ppermute | solution.py:15
  53.1 0.0 copy-start.1
  53.1 22.8 %fusion.60 = bf16[4,6,32,256]{3,1,0,2:T(8,128)(2,1)S(1)} fusion(f32[4,6,32,256]{3,1,0,2:T(8,128)S(1)} %fusion.3, f32[4,6,32,10]{3,1,0,2:T(8,128)S(1)} %collective-permute-done.3, f32[4,6,32,10]{3,1,0,2:T(8,128)S(1)} %collective-permute-done.2, f32[]{:T(128)} %bitcast.44, f32[]{:T(128)} %bitcast.43, f32[]{:T(128)} %bitcast.42, f32[]{:T(128)} %bitcast.41, ...), kind=kLoop, calls=%fused_computation.134 | loop fusion | flops 12189696 | bytes 1241172 | tf_op jit(solution)/shard_map/convert_element_type | solution.py:49
  76.0 0.2 copy.19
  76.2 0.2 copy.26
  76.4 0.0 copy-done.1
  76.4 0.0 copy-start.4
  76.4 1.8 convolution_bitcast_fusion.1
  78.2 114.9 %psum.7 = f32[256,24]{1,0:T(8,128)S(1)} all-reduce(f32[256,24]{1,0:T(8,128)S(1)} %convolution_bitcast_fusion.1), channel_id=1, replica_groups=mesh['gx'=32,'gy'=16] {'gx','gy'}, use_global_device_ids=true, to_apply=%region_0.0 | all-reduce | flops 6144 | bytes 49152 | tf_op jit(solution)/shard_map/psum | solution.py:56
  193.1 0.0 copy-done.4
  193.1 0.6 dynamic-slice_add_fusion
Async XLA Ops:
  0.0 3.1 %copy-start = (f32[6,6]{1,0:T(8,128)S(1)}, f32[6,6]{1,0:T(8,128)}, u32[]{:S(2)}) copy-start(f32[6,6]{1,0:T(8,128)} %param.9) | copy-start | bytes 436
  3.1 6.8 %copy-start.2 = (f32[21]{0:T(128)S(1)}, f32[21]{0:T(128)}, u32[]{:S(2)}) copy-start(f32[21]{0:T(128)} %param.10) | copy-start | bytes 256
  3.1 8.2 %copy-start.3 = (f32[21]{0:T(128)S(1)}, f32[21]{0:T(128)}, u32[]{:S(2)}) copy-start(f32[21]{0:T(128)} %param.11) | copy-start | bytes 256
  4.6 7.9 %collective-permute-start = (f32[4,6,10,256]{3,1,0,2:T(8,128)S(1)}, f32[4,6,10,256]{3,1,0,2:T(8,128)S(1)}, u32[]{:S(2)}, u32[]{:S(2)}) collective-permute-start(f32[4,6,10,256]{3,1,0,2:T(8,128)S(1)} %get-tuple-element.7), channel_id=1, source_target_pairs={{0,16},{16,32},{32,48},{48,64},{64,80},{80,96},{96,112},{112,128},... | collective-permute-start | bytes 737288 | tf_op jit(solution)/shard_map/ppermute | solution.py:12
  8.6 8.0 %collective-permute-start.1 = (f32[4,6,10,256]{3,1,0,2:T(8,128)S(1)}, f32[4,6,10,256]{3,1,0,2:T(8,128)S(1)}, u32[]{:S(2)}, u32[]{:S(2)}) collective-permute-start(f32[4,6,10,256]{3,1,0,2:T(8,128)S(1)} %get-tuple-element.8), channel_id=1, source_target_pairs={{16,0},{32,16},{48,32},{64,48},{80,64},{96,80},{112,96},{128,112},... | collective-permute-start | bytes 737288 | tf_op jit(solution)/shard_map/ppermute | solution.py:15
  32.6 16.2 %collective-permute-start.2 = (f32[4,6,32,10]{3,1,0,2:T(8,128)S(1)}, f32[4,6,32,10]{3,1,0,2:T(8,128)S(1)}, u32[]{:S(2)}, u32[]{:S(2)}) collective-permute-start(f32[4,6,32,10]{3,1,0,2:T(8,128)S(1)} %get-tuple-element.5), channel_id=1, source_target_pairs={{0,1},{1,2},{2,3},{3,4},{4,5},{5,6},{6,7},{7,8},{8,9},{9,10},{10,1... | collective-permute-start | bytes 92168 | tf_op jit(solution)/shard_map/ppermute | solution.py:12
  42.6 10.5 %collective-permute-start.3 = (f32[4,6,32,10]{3,1,0,2:T(8,128)S(1)}, f32[4,6,32,10]{3,1,0,2:T(8,128)S(1)}, u32[]{:S(2)}, u32[]{:S(2)}) collective-permute-start(f32[4,6,32,10]{3,1,0,2:T(8,128)S(1)} %get-tuple-element.6), channel_id=1, source_target_pairs={{1,0},{2,1},{3,2},{4,3},{5,4},{6,5},{7,6},{8,7},{9,8},{10,9},{11,1... | collective-permute-start | bytes 92168 | tf_op jit(solution)/shard_map/ppermute | solution.py:15
  53.1 23.3 %copy-start.1 = (bf16[32,256,256]{2,1,0:T(8,128)(2,1)S(1)}, bf16[32,256,256]{2,1,0:T(8,128)(2,1)}, u32[]{:S(2)}) copy-start(bf16[32,256,256]{2,1,0:T(8,128)(2,1)} %param.12) | copy-start | bytes 12582916
  76.4 116.7 %copy-start.4 = (f32[16,24]{1,0:T(8,128)S(1)}, f32[16,24]{1,0:T(8,128)}, u32[]{:S(2)}) copy-start(f32[16,24]{1,0:T(8,128)} %param.13) | copy-start | bytes 4612
where the time goes:
time: 194 us
  blocking collectives  115 us (59%)
  other arithmetic  39.2 us (20%)
  starting transfers between devices  17.2 us (9%)
  waiting for transfers between devices  12.4 us (6%)
  matrix products  6.28 us (3%)
  local copies, waits for them, and re-layouts  3.52 us (2%)
    psum x1, blocking collectives, local(): total = lax.psum(projection, ('gx', 'gy'))  115 us
    convert_element_type x1, other arithmetic, local(): smoothed = smoothed.astype(jnp.bfloat16)  22.8 us
    add x1, other arithmetic, smooth_valid(): total + taps[j] * lax.slice_in_dim(extended, j, j + count, axis=axis)  15.8 us
    ppermute x2, starting transfers between devices, padded(): lax.ppermute(lax.slice_in_dim(block, block.shape[dim] - width, None, axis...  14 us
    ppermute x2, waiting for transfers between devices, padded(): lax.ppermute(lax.slice_in_dim(block, 0, width, axis=dim), axis, backward)  8.37 us
    dot_general x2, matrix products, local(): jnp.einsum('gf,st,gsxy->ftxy', field_mixing, time_mixing, adjoint_forcing...  4.51 us
    ppermute x2, waiting for transfers between devices, padded(): lax.ppermute(lax.slice_in_dim(block, block.shape[dim] - width, None, axis...  4.06 us
  transfers between devices with their start and end apart: 4, of which 4 were waited for; matrix products, arithmetic and copies ran while one was open for 1% of the time, Pallas kernels for 0%

commit v1 on v0

v1 whole, which is shorter than its diff:
```python
import functools

import jax
import jax.numpy as jnp
from jax import lax
from jax.experimental import pallas as pl
from jax.experimental.pallas import tpu as pltpu
from jax.sharding import PartitionSpec as P

F32, BF16 = jnp.float32, jnp.bfloat16
MESH = pl.DeviceIdType.MESH
C = 24
WX, WY = 32, 256
R = 10
TAPS = 2 * R + 1
MODES = 256
LANES = 128
SLAB = 384
ROW = C
CHUNKS = ((0, 4), (4, 3), (7, 3))


def dot(a, b):
    return jnp.dot(a, b, preferred_element_type=F32)


def split(a):
    high = a.astype(BF16)
    return high, (a - high.astype(F32)).astype(BF16)


def dot3(a, b_high, b_low):
    high, low = split(a)
    return dot(high, b_high) + (dot(high, b_low) + dot(low, b_high))


def iota(shape, dim):
    return lax.broadcasted_iota(jnp.int32, shape, dim)


def band(taps, row0, shift, shape):
    index = iota(shape, 0) - iota(shape, 1) + (row0 + shift)
    out = jnp.zeros(shape, F32)
    for j in range(TAPS):
        out = jnp.where(index == j, taps[j], out)
    return out


def kernel(
    nx, ny,
    adj_hbm, fm_hbm, tm_hbm, ke_hbm, kn_hbm, modes_hbm,
    out_ref,
    adj, modes, fm, tm, ke, kn,
    t_high, t_low, e_high, e_low, y0, ext, part,
    pack_s, pack_r, z_high, z_low, slabs, got_y, got_x,
    load_sem, ysend, yrecv, xsend, xrecv, rs_send, rs_recv, ag_send, ag_recv,
):
    gx, gy = lax.axis_index("gx"), lax.axis_index("gy")
    copy_adj = pltpu.make_async_copy(adj_hbm, adj, load_sem.at[0])
    copy_kn = pltpu.make_async_copy(kn_hbm, kn, load_sem.at[1])
    copy_ke = pltpu.make_async_copy(ke_hbm, ke, load_sem.at[2])
    copy_fm = pltpu.make_async_copy(fm_hbm, fm, load_sem.at[3])
    copy_tm = pltpu.make_async_copy(tm_hbm, tm, load_sem.at[4])
    copy_modes = pltpu.make_async_copy(modes_hbm, modes, load_sem.at[5])
    for copy in (copy_adj, copy_kn, copy_ke, copy_fm, copy_tm, copy_modes):
        copy.start()

    barrier = pltpu.get_barrier_semaphore()

    @pl.loop(1, ny)
    def _(d):
        pl.semaphore_signal(
            barrier, inc=1, device_id={"gy": lax.rem(gy + d, ny)}, device_id_type=MESH
        )

    @pl.loop(1, nx)
    def _(d):
        pl.semaphore_signal(
            barrier, inc=1, device_id={"gx": lax.rem(gx + d, nx)}, device_id_type=MESH
        )

    copy_kn.wait()
    for i in range(0, WY, 16):
        for h in range(0, WY, LANES):
            rows = (pl.ds(i, 16), pl.ds(h, LANES))
            if i - R > h + LANES - 1 or i + 15 + R < h:
                t_high[rows] = jnp.zeros((16, LANES), BF16)
                t_low[rows] = jnp.zeros((16, LANES), BF16)
            else:
                t_high[rows], t_low[rows] = split(band(kn, i - h, R, (16, LANES)))
    zeros = jnp.zeros((16, LANES), BF16)
    edge_row = iota((16, LANES), 0) < R
    e_high[...] = jnp.zeros_like(e_high)
    e_low[...] = jnp.zeros_like(e_low)
    low_side = jnp.where(edge_row, band(kn, 0, 0, (16, LANES)), 0.0)
    e_high[0:16, 0:LANES], e_low[0:16, 0:LANES] = split(low_side)
    high_side = jnp.where(edge_row, band(kn, WY - LANES, R, (16, LANES)), 0.0)
    e_high[16:32, LANES:WY], e_low[16:32, LANES:WY] = split(high_side)

    copy_adj.wait()
    lane = iota((64, LANES), 1)
    pack_low = jnp.zeros((64, LANES), F32)
    pack_high = jnp.zeros((64, LANES), F32)
    for b in range(12):
        here = (lane >= R * b) & (lane < R * (b + 1))
        low = adj[2 * b : 2 * b + 2, :, 0:LANES].reshape(64, LANES)
        high = adj[2 * b : 2 * b + 2, :, LANES:WY].reshape(64, LANES)
        if b:
            low = pltpu.roll(low, R * b, 1)
        high = pltpu.roll(high, (R * b + R) % LANES, 1)
        pack_low = jnp.where(here, low, pack_low)
        pack_high = jnp.where(here, high, pack_high)
    pack_s[0] = pack_low
    pack_s[1] = pack_high

    pl.semaphore_wait(barrier, nx + ny - 2)

    to_south = pltpu.make_async_remote_copy(
        pack_s.at[0], pack_r.at[1], ysend.at[0], yrecv.at[1],
        device_id={"gy": jnp.maximum(gy - 1, 0)}, device_id_type=MESH,
    )
    to_north = pltpu.make_async_remote_copy(
        pack_s.at[1], pack_r.at[0], ysend.at[1], yrecv.at[0],
        device_id={"gy": jnp.minimum(gy + 1, ny - 1)}, device_id_type=MESH,
    )

    @pl.when(gy > 0)
    def _():
        to_south.start()

    @pl.when(gy < ny - 1)
    def _():
        to_north.start()

    for q in range(3):
        tile = adj[8 * q : 8 * q + 8].reshape(256, WY)
        y0[256 * q : 256 * q + 256, :] = dot3(tile, t_high[...], t_low[...])

    @pl.when(gy > 0)
    def _():
        to_north.wait_recv()

    @pl.when(gy == 0)
    def _():
        pack_r[0] = jnp.zeros((64, LANES), F32)

    @pl.when(gy < ny - 1)
    def _():
        to_south.wait_recv()

    @pl.when(gy == ny - 1)
    def _():
        pack_r[1] = jnp.zeros((64, LANES), F32)

    from_low, from_high = pack_r[0], pack_r[1]
    for q in range(3):
        pieces = []
        for b in range(4 * q, 4 * q + 4):
            low = pltpu.roll(from_low, (LANES - R * b) % LANES, 1) if b else from_low
            high = pltpu.roll(from_high, (LANES + 16 - R * b) % LANES, 1)
            pieces.append(jnp.where(lane < 16, low, high))
        extra = jnp.concatenate(pieces, axis=0)
        total = y0[256 * q : 256 * q + 256, :] + dot3(extra, e_high[...], e_low[...])
        for c in range(8):
            rows = pl.ds(R * ROW + 8 * q + c, WX, stride=ROW)
            ext[0, rows, :] = total[32 * c : 32 * c + 32, :LANES]
            ext[1, rows, :] = total[32 * c : 32 * c + 32, LANES:]

    west, east = jnp.maximum(gx - 1, 0), jnp.minimum(gx + 1, nx - 1)
    to_west, to_east = [], []
    for k, (first, count) in enumerate(CHUNKS):
        rows = count * ROW
        to_west.append(
            pltpu.make_async_remote_copy(
                ext.at[:, pl.ds((R + first) * ROW, rows)],
                ext.at[:, pl.ds((R + WX + first) * ROW, rows)],
                xsend.at[k], xrecv.at[k],
                device_id={"gx": west}, device_id_type=MESH,
            )
        )
        to_east.append(
            pltpu.make_async_remote_copy(
                ext.at[:, pl.ds((R + WX - first - count) * ROW, rows)],
                ext.at[:, pl.ds((R - first - count) * ROW, rows)],
                xsend.at[3 + k], xrecv.at[3 + k],
                device_id={"gx": east}, device_id_type=MESH,
            )
        )
    for k in range(len(CHUNKS)):

        @pl.when(gx > 0)
        def _():
            to_west[k].start()

        @pl.when(gx < nx - 1)
        def _():
            to_east[k].start()

    copy_fm.wait()
    copy_tm.wait()
    copy_ke.wait()
    row, col = iota((C, LANES), 0), iota((C, LANES), 1)
    field_part = jnp.zeros((C, LANES), F32)
    for g in range(4):
        for f in range(4):
            chosen = (row // 6 == g) & (col // 6 == f)
            field_part = jnp.where(chosen, fm[g, f], field_part)
    time_part = jnp.zeros((C, LANES), F32)
    for s in range(6):
        for t in range(6):
            chosen = (row % 6 == s) & (col % 6 == t)
            time_part = jnp.where(chosen, tm[s, t], time_part)
    mix = field_part * time_part
    group = lax.rem(gy, 8)
    lane_of = iota((SLAB, C), 0)
    channel = 8 * (lane_of // LANES) + lax.rem(group + 8 - (lane_of % LANES) // 16, 8)
    pick = (channel == iota((SLAB, C), 1)).astype(F32)
    mixing = jnp.dot(pick, mix, preferred_element_type=F32, precision=lax.Precision.HIGHEST)
    z_high[...], z_low[...] = split(mixing)

    def column(start):
        return jnp.concatenate([ext[h, pl.ds(start, ROW), :] for h in range(2)], axis=1)

    def columns(start, count, first_tap):
        total = ke[first_tap] * column(start)
        for j in range(1, count):
            total = total + ke[first_tap + j] * column(start + j * ROW)
        return total

    def project(total, x):
        low = total - total.astype(BF16).astype(F32)
        both = jnp.concatenate([total, low], axis=0).astype(BF16)
        return dot(both, modes[x])

    copy_modes.wait()

    def interior(x, acc):
        start = pl.multiple_of(x * ROW, 8)
        return acc + project(columns(start, TAPS, 0), x)

    acc = lax.fori_loop(R, WX - R, interior, jnp.zeros((2 * C, MODES), F32))

    for e in range(R):
        part[e] = columns(R * ROW, e + R + 1, R - e)
        part[R + e] = columns((WX - 1 - e) * ROW, e + R + 1, 0)

    @pl.when(gx == 0)
    def _():
        ext[:, 0 : R * ROW, :] = jnp.zeros((2, R * ROW, LANES), F32)

    @pl.when(gx == nx - 1)
    def _():
        ext[:, (R + WX) * ROW : (2 * R + WX) * ROW, :] = jnp.zeros((2, R * ROW, LANES), F32)

    for k, (first, count) in enumerate(CHUNKS):

        @pl.when(gx > 0)
        def _():
            to_east[k].wait_recv()

        @pl.when(gx < nx - 1)
        def _():
            to_west[k].wait_recv()

        last = first + count
        for e in range(R - first):
            low, high = part[e], part[R + e]
            for d in range(first + 1, min(last, R - e) + 1):
                low = low + ke[R - d - e] * column((R - d) * ROW)
                high = high + ke[R + d + e] * column((R + WX - 1 + d) * ROW)
            if R - e <= last:
                acc = acc + project(low, e)
                acc = acc + project(high, WX - 1 - e)
            else:
                part[e] = low
                part[R + e] = high

    total = acc[:C] + acc[C:]

    sub, lanes = iota((8, LANES), 0), iota((8, LANES), 1) // 16
    for r in range(3):
        for h in range(2):
            v = total[8 * r : 8 * r + 8, LANES * h : LANES * h + LANES]
            for bit in (1, 2, 4):
                v = jnp.where((sub & bit) != 0, pltpu.roll(v, LANES - 16 * bit, 1), v)
            for bit in (1, 2, 4):
                v = jnp.where((lanes & bit) != 0, pltpu.roll(v, bit, 0), v)
            for g in range(8):
                slabs[8 * h + g, :, LANES * r : LANES * r + LANES] = v[g : g + 1]

    @pl.loop(1, ny)
    def _(d):
        peer = lax.rem(gy + d, ny)
        pltpu.make_async_remote_copy(
            slabs.at[peer], got_y.at[d - 1], rs_send, rs_recv,
            device_id={"gy": peer}, device_id_type=MESH,
        ).start()

    mine = slabs[gy]
    pltpu.make_async_copy(got_y, got_y, rs_recv).wait()
    for d in range(ny - 1):
        mine = mine + got_y[d]
    got_x[gx] = mine

    @pl.loop(1, nx)
    def _(d):
        peer = lax.rem(gx + d, nx)
        pltpu.make_async_remote_copy(
            got_x.at[gx], got_x.at[gx], ag_send, ag_recv,
            device_id={"gx": peer}, device_id_type=MESH,
        ).start()

    others = got_x.at[pl.ds(0, nx - 1)]
    pltpu.make_async_copy(others, others, ag_recv).wait()
    whole = got_x[0]
    for d in range(1, nx):
        whole = whole + got_x[d]

    shape = (16, SLAB)
    spread = jnp.where(
        iota(shape, 1) % 16 == iota(shape, 0), jnp.broadcast_to(whole, shape), 0.0
    )
    out_ref[...] = dot3(spread, z_high[...], z_low[...])[:, :C]

    @pl.when(gy > 0)
    def _():
        to_south.wait_send()

    @pl.when(gy < ny - 1)
    def _():
        to_north.wait_send()

    for k in range(len(CHUNKS)):

        @pl.when(gx > 0)
        def _():
            to_west[k].wait_send()

        @pl.when(gx < nx - 1)
        def _():
            to_east[k].wait_send()

    pltpu.make_async_copy(got_y, got_y, rs_send).wait()
    pltpu.make_async_copy(others, others, ag_send).wait()


def solution(mesh):
    nx, ny = mesh.shape["gx"], mesh.shape["gy"]

    def local(adj, field_mixing, time_mixing, kernel_east, kernel_north, modes, coefficients):
        vmem, smem, dma = pltpu.VMEM, pltpu.SMEM, pltpu.SemaphoreType.DMA
        projection = pl.pallas_call(
            functools.partial(kernel, nx, ny),
            out_shape=jax.ShapeDtypeStruct((MODES // ny, C), F32),
            in_specs=[pl.BlockSpec(memory_space=pl.ANY)] * 6,
            out_specs=pl.BlockSpec(memory_space=pltpu.VMEM),
            scratch_shapes=[
                vmem((C, WX, WY), F32),
                vmem((WX, WY, MODES), BF16),
                smem((4, 4), F32),
                smem((6, 6), F32),
                smem((TAPS,), F32),
                smem((TAPS,), F32),
                vmem((WY, WY), BF16),
                vmem((WY, WY), BF16),
                vmem((LANES, WY), BF16),
                vmem((LANES, WY), BF16),
                vmem((C * WX, WY), F32),
                vmem((2, (WX + 2 * R) * ROW, LANES), F32),
                vmem((2 * R, C, WY), F32),
                vmem((2, 64, LANES), F32),
                vmem((2, 64, LANES), F32),
                vmem((SLAB, LANES), BF16),
                vmem((SLAB, LANES), BF16),
                vmem((ny, 1, SLAB), F32),
                vmem((ny - 1, 1, SLAB), F32),
                vmem((nx, 1, SLAB), F32),
                dma((6,)),
                dma((2,)),
                dma((2,)),
                dma((6,)),
                dma((6,)),
                dma,
                dma,
                dma,
                dma,
            ],
            compiler_params=pltpu.CompilerParams(
                collective_id=0, has_side_effects=True, vmem_limit_bytes=40 << 20
            ),
            name="gradient",
        )(
            adj.reshape(C, WX, WY), field_mixing, time_mixing,
            kernel_east, kernel_north, modes,
        )
        return coefficients + projection

    in_specs = (P(None, None, "gx", "gy"), P(), P(), P(), P(), P("gx", "gy", None), P("gy", None))
    return jax.shard_map(
        local, mesh=mesh, in_specs=in_specs, out_specs=P("gy", None), check_vma=False
    )
```

time: 194 us -> 52.1 us (0.27)
  blocking collectives: 115 us -> 0 us
  Pallas kernels: 0 us -> 45.2 us
  other arithmetic: 39.2 us -> 0.6 us
  starting transfers between devices: 17.2 us -> 0 us
  waiting for transfers between devices: 12.4 us -> 0 us
  matrix products: 6.28 us -> 0 us
  local copies, waits for them, and re-layouts: 3.52 us -> 6 us
    psum x1 -> x0, blocking collectives: 115 us -> none  [local(): total = lax.psum(projection, ('gx', 'gy'))]
    pallas_call x0 -> x1, Pallas kernels: none -> 45.2 us  [local(): pl.pallas_call(functools.partial(kernel, nx, ny), out_shape=jax.ShapeDtyp...]
    convert_element_type x1 -> x0, other arithmetic: 22.8 us -> none  [local(): smoothed = smoothed.astype(jnp.bfloat16)]
    ppermute x4 -> x0, starting transfers between devices: 17.2 us -> none  [the longest x2 14 us: padded(): lax.ppermute(lax.slice_in_dim(block, block.shape[dim] - width, None, axis...]
    add x2 -> x1, other arithmetic: 16.4 us -> 0.6 us  [local(): return coefficients + projection]
    ppermute x4 -> x0, waiting for transfers between devices: 12.4 us -> none  [the longest x2 8.37 us: padded(): lax.ppermute(lax.slice_in_dim(block, 0, width, axis=dim), axis, backward)]
    dot_general x3 -> x0, matrix products: 6.28 us -> none  [the longest x2 4.51 us: local(): jnp.einsum('gf,st,gsxy->ftxy', field_mixing, time_mixing, adjoint_forcing...]
    unnamed x11 -> x14, local copies, waits for them, and re-layouts: 0.25 us -> 6 us
  transfers between devices with their start and end apart: 4 -> 0, of which waited for: 4 -> 0; matrix products, arithmetic and copies ran while one was open for 1% -> 0% of each run, Pallas kernels for 0% -> 0%
where the time goes in v1:
time: 52.1 us; the launch traced here: 51.8 us
  Pallas kernels  45.2 us (87%)
  local copies, waits for them, and re-layouts  6 us (12%)
  other arithmetic  0.6 us (1%)
    pallas_call x1, Pallas kernels, local(): pl.pallas_call(functools.partial(kernel, nx, ny), out_shape=jax.ShapeDtyp...  45.2 us
    unnamed x14, local copies, waits for them, and re-layouts  6 us

profile of v1, /device:TPU:1, one launch (start us, length us, event | category | flops | bytes accessed | tf_op | source)
XLA Modules:
  0.0 51.8 jit_solution(8865558256777091751)
XLA Ops:
  0.0 0.0 copy-start
  0.0 2.2 %copy-done = bf16[32,256,256]{2,1,0:T(8,128)(2,1)S(1)} copy-done((bf16[32,256,256]{2,1,0:T(8,128)(2,1)S(1)}, bf16[32,256,256]{2,1,0:T(8,128)(2,1)}, u32[]{:S(2)}) %copy-start) | copy-done | bytes 4194328
  2.2 0.0 copy-start.1
  2.2 1.1 %copy-done.1 = f32[4,6,32,256]{3,2,1,0:T(8,128)S(1)} copy-done((f32[4,6,32,256]{3,2,1,0:T(8,128)S(1)}, f32[4,6,32,256]{3,2,1,0:T(8,128)}, u32[]{:S(2)}) %copy-start.1) | copy-done | bytes 786456
  3.3 0.0 copy-start.2
  3.3 0.7 %copy-done.2 = f32[6,6]{1,0:T(8,128)S(1)} copy-done((f32[6,6]{1,0:T(8,128)S(1)}, f32[6,6]{1,0:T(8,128)}, u32[]{:S(2)}) %copy-start.2) | copy-done | bytes 168
  4.0 0.0 copy-start.3
  4.0 0.7 %copy-done.3 = f32[4,4]{1,0:T(4,128)S(1)} copy-done((f32[4,4]{1,0:T(4,128)S(1)}, f32[4,4]{1,0:T(4,128)}, u32[]{:S(2)}) %copy-start.3) | copy-done | bytes 88
  4.7 0.0 copy-start.4
  4.7 0.7 %copy-done.4 = f32[21]{0:T(128)S(1)} copy-done((f32[21]{0:T(128)S(1)}, f32[21]{0:T(128)}, u32[]{:S(2)}) %copy-start.4) | copy-done | bytes 108
  5.3 0.0 copy-start.5
  5.3 0.7 %copy-done.5 = f32[21]{0:T(128)S(1)} copy-done((f32[21]{0:T(128)S(1)}, f32[21]{0:T(128)}, u32[]{:S(2)}) %copy-start.5) | copy-done | bytes 108
  6.0 0.0 copy-start.6
  6.0 45.2 %gradient.1 = f32[16,24]{1,0:T(8,128)S(1)} custom-call(f32[24,32,256]{2,1,0:T(8,128)S(1)} %bitcast.1, f32[4,4]{1,0:T(4,128)S(1)} %copy-done.3, f32[6,6]{1,0:T(8,128)S(1)} %copy-done.2, f32[21]{0:T(128)S(1)} %copy-done.4, f32[21]{0:T(128)S(1)} %copy-done.5, bf16[32,256,256]{2,1,0:T(8,128)(2,1)S(1)} %copy-done), custom_call_target="tpu_custom_call" | custom-call | tf_op jit(solution)/shard_map/gradient/pallas_call | solution.py:352
  51.2 0.0 copy-done.6
  51.2 0.6 %add.3 = f32[16,24]{1,0:T(8,128)} add(f32[16,24]{1,0:T(8,128)S(1)} %copy-done.6, f32[16,24]{1,0:T(8,128)S(1)} %gradient.1) | non-fusion elementwise | flops 384 | bytes 4608 | tf_op jit(solution)/shard_map/add | solution.py:396
Async XLA Ops:
  0.0 2.2 %copy-start = (bf16[32,256,256]{2,1,0:T(8,128)(2,1)S(1)}, bf16[32,256,256]{2,1,0:T(8,128)(2,1)}, u32[]{:S(2)}) copy-start(bf16[32,256,256]{2,1,0:T(8,128)(2,1)} %modes_hbm.1) | copy-start | bytes 12582916
  2.2 1.1 %copy-start.1 = (f32[4,6,32,256]{3,2,1,0:T(8,128)S(1)}, f32[4,6,32,256]{3,2,1,0:T(8,128)}, u32[]{:S(2)}) copy-start(f32[4,6,32,256]{3,2,1,0:T(8,128)} %param.7) | copy-start | bytes 2359300
  3.3 0.7 %copy-start.2 = (f32[6,6]{1,0:T(8,128)S(1)}, f32[6,6]{1,0:T(8,128)}, u32[]{:S(2)}) copy-start(f32[6,6]{1,0:T(8,128)} %tm_hbm.1) | copy-start | bytes 436
  4.0 0.7 %copy-start.3 = (f32[4,4]{1,0:T(4,128)S(1)}, f32[4,4]{1,0:T(4,128)}, u32[]{:S(2)}) copy-start(f32[4,4]{1,0:T(4,128)} %fm_hbm.1) | copy-start | bytes 196
  4.7 0.7 %copy-start.4 = (f32[21]{0:T(128)S(1)}, f32[21]{0:T(128)}, u32[]{:S(2)}) copy-start(f32[21]{0:T(128)} %ke_hbm.1) | copy-start | bytes 256
  5.3 0.7 %copy-start.5 = (f32[21]{0:T(128)S(1)}, f32[21]{0:T(128)}, u32[]{:S(2)}) copy-start(f32[21]{0:T(128)} %kn_hbm.1) | copy-start | bytes 256
  6.0 45.2 %copy-start.6 = (f32[16,24]{1,0:T(8,128)S(1)}, f32[16,24]{1,0:T(8,128)}, u32[]{:S(2)}) copy-start(f32[16,24]{1,0:T(8,128)} %param.13) | copy-start | bytes 4612

commit v2 on v1

--- a/solution.py
+++ b/solution.py
@@ -17,7 +17,8 @@
 LANES = 128
 SLAB = 384
 ROW = C
-CHUNKS = ((0, 4), (4, 3), (7, 3))
+NEAR = 4
+CHUNKS = ((0, NEAR), (4, 3), (7, 3))
 
 
 def dot(a, b):
@@ -52,8 +53,8 @@
     out_ref,
     adj, modes, fm, tm, ke, kn,
     t_high, t_low, e_high, e_low, y0, ext, part,
-    pack_s, pack_r, z_high, z_low, slabs, got_y, got_x,
-    load_sem, ysend, yrecv, xsend, xrecv, rs_send, rs_recv, ag_send, ag_recv,
+    pack_s, pack_r, raw_s, raw_r, corner_s, corner_r, z_high, z_low, slabs, got_y, got_x,
+    load_sem, ysend, yrecv, xsend, xrecv, csend, crecv, rs_send, rs_recv, ag_send, ag_recv,
 ):
     gx, gy = lax.axis_index("gx"), lax.axis_index("gy")
     copy_adj = pltpu.make_async_copy(adj_hbm, adj, load_sem.at[0])
@@ -62,22 +63,35 @@
     copy_fm = pltpu.make_async_copy(fm_hbm, fm, load_sem.at[3])
     copy_tm = pltpu.make_async_copy(tm_hbm, tm, load_sem.at[4])
     copy_modes = pltpu.make_async_copy(modes_hbm, modes, load_sem.at[5])
-    for copy in (copy_adj, copy_kn, copy_ke, copy_fm, copy_tm, copy_modes):
+    for copy in (copy_adj, copy_kn, copy_ke, copy_fm, copy_tm):
         copy.start()
 
     barrier = pltpu.get_barrier_semaphore()
 
-    @pl.loop(1, ny)
-    def _(d):
-        pl.semaphore_signal(
-            barrier, inc=1, device_id={"gy": lax.rem(gy + d, ny)}, device_id_type=MESH
-        )
-
-    @pl.loop(1, nx)
-    def _(d):
-        pl.semaphore_signal(
-            barrier, inc=1, device_id={"gx": lax.rem(gx + d, nx)}, device_id_type=MESH
-        )
+    def greet(there):
+        pl.semaphore_signal(barrier, inc=1, device_id=there, device_id_type=MESH)
+
+    west, east = jnp.maximum(gx - 1, 0), jnp.minimum(gx + 1, nx - 1)
+    south, north = jnp.maximum(gy - 1, 0), jnp.minimum(gy + 1, ny - 1)
+    has_x = (gx > 0, gx < nx - 1)
+    has_y = (gy > 0, gy < ny - 1)
+    diagonal = [
+        (2 * i + j, has_x[i] & has_y[j], {"gx": (west, east)[i], "gy": (south, north)[j]})
+        for i in range(2)
+        for j in range(2)
+    ]
+    for d in range(1, nx):
+        greet({"gx": gx ^ d})
+    for d in range(1, ny):
+        greet({"gy": gy ^ d})
+    greeted = nx + ny - 2
+    for i, there, device in diagonal:
+
+        @pl.when(there)
+        def _():
+            greet(device)
+
+        greeted = greeted + there.astype(jnp.int32)
 
     copy_kn.wait()
     for i in range(0, WY, 16):
@@ -88,7 +102,6 @@
                 t_low[rows] = jnp.zeros((16, LANES), BF16)
             else:
                 t_high[rows], t_low[rows] = split(band(kn, i - h, R, (16, LANES)))
-    zeros = jnp.zeros((16, LANES), BF16)
     edge_row = iota((16, LANES), 0) < R
     e_high[...] = jnp.zeros_like(e_high)
     e_low[...] = jnp.zeros_like(e_low)
@@ -98,6 +111,7 @@
     e_high[16:32, LANES:WY], e_low[16:32, LANES:WY] = split(high_side)
 
     copy_adj.wait()
+    copy_modes.start()
     lane = iota((64, LANES), 1)
     pack_low = jnp.zeros((64, LANES), F32)
     pack_high = jnp.zeros((64, LANES), F32)
@@ -113,15 +127,15 @@
     pack_s[0] = pack_low
     pack_s[1] = pack_high
 
-    pl.semaphore_wait(barrier, nx + ny - 2)
+    pl.semaphore_wait(barrier, greeted)
 
     to_south = pltpu.make_async_remote_copy(
         pack_s.at[0], pack_r.at[1], ysend.at[0], yrecv.at[1],
-        device_id={"gy": jnp.maximum(gy - 1, 0)}, device_id_type=MESH,
+        device_id={"gy": south}, device_id_type=MESH,
     )
     to_north = pltpu.make_async_remote_copy(
         pack_s.at[1], pack_r.at[0], ysend.at[1], yrecv.at[0],
-        device_id={"gy": jnp.minimum(gy + 1, ny - 1)}, device_id_type=MESH,
+        device_id={"gy": north}, device_id_type=MESH,
     )
 
     @pl.when(gy > 0)
@@ -131,6 +145,51 @@
     @pl.when(gy < ny - 1)
     def _():
         to_north.start()
+
+    for side, first in enumerate((0, WX - 8)):
+        for c in range(C):
+            edge = adj[c, first : first + 8, :]
+            for h in range(2):
+                raw_s[side, h, pl.ds(c, 8, stride=ROW), :] = edge[:, LANES * h : LANES * h + LANES]
+
+    near = NEAR * ROW
+    raw_west = pltpu.make_async_remote_copy(
+        raw_s.at[0, :, pl.ds(0, near)], raw_r.at[1], xsend.at[0], xrecv.at[0],
+        device_id={"gx": west}, device_id_type=MESH,
+    )
+    raw_east = pltpu.make_async_remote_copy(
+        raw_s.at[1, :, pl.ds(near, near)], raw_r.at[0], xsend.at[3], xrecv.at[3],
+        device_id={"gx": east}, device_id_type=MESH,
+    )
+
+    @pl.when(gx > 0)
+    def _():
+        raw_west.start()
+
+    @pl.when(gx < nx - 1)
+    def _():
+        raw_east.start()
+
+    lane8 = iota((8, LANES), 1)
+    corners = []
+    for i in range(2):
+        for j in range(2):
+            packed = jnp.zeros((8, LANES), F32)
+            for b in range(12):
+                piece = raw_s[i, j, near * i + 8 * b : near * i + 8 * b + 8, :]
+                piece = pltpu.roll(piece, (R * b + R * j) % LANES, 1) if b + j else piece
+                packed = jnp.where((lane8 >= R * b) & (lane8 < R * (b + 1)), piece, packed)
+            corner_s[2 * i + j] = packed
+    for k, there, device in diagonal:
+        copy = pltpu.make_async_remote_copy(
+            corner_s.at[k], corner_r.at[3 - k], csend.at[k], crecv.at[3 - k],
+            device_id=device, device_id_type=MESH,
+        )
+        corners.append(copy)
+
+        @pl.when(there)
+        def _():
+            copy.start()
 
     for q in range(3):
         tile = adj[8 * q : 8 * q + 8].reshape(256, WY)
@@ -166,9 +225,10 @@
             ext[0, rows, :] = total[32 * c : 32 * c + 32, :LANES]
             ext[1, rows, :] = total[32 * c : 32 * c + 32, LANES:]
 
-    west, east = jnp.maximum(gx - 1, 0), jnp.minimum(gx + 1, nx - 1)
-    to_west, to_east = [], []
+    to_west, to_east = [raw_west], [raw_east]
     for k, (first, count) in enumerate(CHUNKS):
+        if not k:
+            continue
         rows = count * ROW
         to_west.append(
             pltpu.make_async_remote_copy(
@@ -186,7 +246,7 @@
                 device_id={"gx": east}, device_id_type=MESH,
             )
         )
-    for k in range(len(CHUNKS)):
+    for k in range(1, len(CHUNKS)):
 
         @pl.when(gx > 0)
         def _():
@@ -262,6 +322,35 @@
         def _():
             to_west[k].wait_recv()
 
+        if not k:
+            for i, there, device in diagonal:
+
+                @pl.when(there)
+                def _():
+                    corners[3 - i].wait_recv()
+
+                @pl.when(jnp.logical_not(there))
+                def _():
+                    corner_r[i] = jnp.zeros((8, LANES), F32)
+
+            for side in range(2):
+
+                @pl.when(has_x[side])
+                def _():
+                    low, high = corner_r[2 * side], corner_r[2 * side + 1]
+                    pieces = []
+                    for b in range(12):
+                        a = pltpu.roll(low, (LANES - R * b) % LANES, 1) if b else low
+                        c = pltpu.roll(high, (LANES + 16 - R * b) % LANES, 1)
+                        pieces.append(jnp.where(lane8 < 16, a, c))
+                    extra = jnp.concatenate(pieces, axis=0)
+                    tile = jnp.concatenate([raw_r[side, 0], raw_r[side, 1]], axis=1)
+                    done = dot3(tile, t_high[...], t_low[...])
+                    done = done + dot3(extra, e_high[...], e_low[...])
+                    at = (R - NEAR) * ROW if side == 0 else (R + WX) * ROW
+                    ext[0, pl.ds(at, near), :] = done[:, :LANES]
+                    ext[1, pl.ds(at, near), :] = done[:, LANES:]
+
         last = first + count
         for e in range(R - first):
             low, high = part[e], part[R + e]
@@ -288,9 +377,8 @@
             for g in range(8):
                 slabs[8 * h + g, :, LANES * r : LANES * r + LANES] = v[g : g + 1]
 
-    @pl.loop(1, ny)
-    def _(d):
-        peer = lax.rem(gy + d, ny)
+    for d in sorted(range(1, ny), key=lambda d: -2 * (d & 12).bit_count() - (d & 3).bit_count()):
+        peer = gy ^ d
         pltpu.make_async_remote_copy(
             slabs.at[peer], got_y.at[d - 1], rs_send, rs_recv,
             device_id={"gy": peer}, device_id_type=MESH,
@@ -302,13 +390,14 @@
         mine = mine + got_y[d]
     got_x[gx] = mine
 
-    @pl.loop(1, nx)
-    def _(d):
-        peer = lax.rem(gx + d, nx)
-        pltpu.make_async_remote_copy(
-            got_x.at[gx], got_x.at[gx], ag_send, ag_recv,
-            device_id={"gx": peer}, device_id_type=MESH,
-        ).start()
+    for peer in range(nx):
+
+        @pl.when(gx != peer)
+        def _():
+            pltpu.make_async_remote_copy(
+                got_x.at[gx], got_x.at[gx], ag_send, ag_recv,
+                device_id={"gx": peer}, device_id_type=MESH,
+            ).start()
 
     others = got_x.at[pl.ds(0, nx - 1)]
     pltpu.make_async_copy(others, others, ag_recv).wait()
@@ -340,6 +429,12 @@
         def _():
             to_east[k].wait_send()
 
+    for k, there, device in diagonal:
+
+        @pl.when(there)
+        def _():
+            corners[k].wait_send()
+
     pltpu.make_async_copy(got_y, got_y, rs_send).wait()
     pltpu.make_async_copy(others, others, ag_send).wait()
 
@@ -352,7 +447,7 @@
         projection = pl.pallas_call(
             functools.partial(kernel, nx, ny),
             out_shape=jax.ShapeDtypeStruct((MODES // ny, C), F32),
-            in_specs=[pl.BlockSpec(memory_space=pl.ANY)] * 6,
+            in_specs=[pl.BlockSpec(memory_space=pltpu.HBM)] * 6,
             out_specs=pl.BlockSpec(memory_space=pltpu.VMEM),
             scratch_shapes=[
                 vmem((C, WX, WY), F32),
@@ -370,6 +465,10 @@
                 vmem((2 * R, C, WY), F32),
                 vmem((2, 64, LANES), F32),
                 vmem((2, 64, LANES), F32),
+                vmem((2, 2, 8 * ROW, LANES), F32),
+                vmem((2, 2, NEAR * ROW, LANES), F32),
+                vmem((4, 8, LANES), F32),
+                vmem((4, 8, LANES), F32),
                 vmem((SLAB, LANES), BF16),
                 vmem((SLAB, LANES), BF16),
                 vmem((ny, 1, SLAB), F32),
@@ -380,13 +479,15 @@
                 dma((2,)),
                 dma((6,)),
                 dma((6,)),
+                dma((4,)),
+                dma((4,)),
                 dma,
                 dma,
                 dma,
                 dma,
             ],
             compiler_params=pltpu.CompilerParams(
-                collective_id=0, has_side_effects=True, vmem_limit_bytes=40 << 20
+                collective_id=0, has_side_effects=True
             ),
             name="gradient",
         )(

time: 52.1 us -> 43.8 us (0.84)
  local copies, waits for them, and re-layouts: 6 us -> 0.01 us
  Pallas kernels: 45.2 us -> 42.2 us
  other arithmetic: 0.6 us -> 1.3 us
    unnamed x14 -> x2, local copies, waits for them, and re-layouts: 6 us -> 0.01 us
    pallas_call x1, Pallas kernels: 45.2 us -> 42.2 us  [local(): pl.pallas_call(functools.partial(kernel, nx, ny), out_shape=jax.ShapeDtyp...]
    add x1, other arithmetic: 0.6 us -> 1.3 us  [local(): return coefficients + projection]
where the time goes in v2:
time: 43.8 us; the launch traced here: 43.6 us
  Pallas kernels  42.2 us (96%)
  other arithmetic  1.3 us (3%)
    pallas_call x1, Pallas kernels, local(): pl.pallas_call(functools.partial(kernel, nx, ny), out_shape=jax.ShapeDtyp...  42.2 us
    add x1, other arithmetic, local(): return coefficients + projection  1.3 us

profile of v2, /device:TPU:1, one launch (start us, length us, event | category | flops | bytes accessed | tf_op | source)
XLA Modules:
  0.0 43.6 jit_solution(2696288474837919262)
XLA Ops:
  0.0 0.0 copy-start
  0.0 42.2 %gradient.1 = f32[16,24]{1,0:T(8,128)} custom-call(f32[24,32,256]{2,1,0:T(8,128)} %bitcast.1, f32[4,4]{1,0:T(4,128)} %fm_hbm.1, f32[6,6]{1,0:T(8,128)} %tm_hbm.1, f32[21]{0:T(128)} %ke_hbm.1, f32[21]{0:T(128)} %kn_hbm.1, bf16[32,256,256]{2,1,0:T(8,128)(2,1)} %modes_hbm.1), custom_call_target="tpu_custom_call" | custom-call | tf_op jit(solution)/shard_map/gradient/pallas_call | solution.py:447
  42.2 0.0 copy-done
  42.3 1.3 %add.3 = f32[16,24]{1,0:T(8,128)} add(f32[16,24]{1,0:T(8,128)S(1)} %copy-done, f32[16,24]{1,0:T(8,128)} %gradient.1) | non-fusion elementwise | flops 384 | bytes 4608 | tf_op jit(solution)/shard_map/add | solution.py:497
Async XLA Ops:
  0.0 42.2 %copy-start = (f32[16,24]{1,0:T(8,128)S(1)}, f32[16,24]{1,0:T(8,128)}, u32[]{:S(2)}) copy-start(f32[16,24]{1,0:T(8,128)} %param.13) | copy-start | bytes 4612

commit v3 on v2

--- a/solution.py
+++ b/solution.py
@@ -127,6 +127,12 @@
     pack_s[0] = pack_low
     pack_s[1] = pack_high
 
+    for side, first in enumerate((0, WX - 8)):
+        for c in range(C):
+            edge = adj[c, first : first + 8, :]
+            for h in range(2):
+                raw_s[side, h, pl.ds(c, 8, stride=ROW), :] = edge[:, LANES * h : LANES * h + LANES]
+
     pl.semaphore_wait(barrier, greeted)
 
     to_south = pltpu.make_async_remote_copy(
@@ -145,12 +151,6 @@
     @pl.when(gy < ny - 1)
     def _():
         to_north.start()
-
-    for side, first in enumerate((0, WX - 8)):
-        for c in range(C):
-            edge = adj[c, first : first + 8, :]
-            for h in range(2):
-                raw_s[side, h, pl.ds(c, 8, stride=ROW), :] = edge[:, LANES * h : LANES * h + LANES]
 
     near = NEAR * ROW
     raw_west = pltpu.make_async_remote_copy(
@@ -444,6 +444,9 @@
 
     def local(adj, field_mixing, time_mixing, kernel_east, kernel_north, modes, coefficients):
         vmem, smem, dma = pltpu.VMEM, pltpu.SMEM, pltpu.SemaphoreType.DMA
+        operands = (
+            adj.reshape(C, WX, WY), field_mixing, time_mixing, kernel_east, kernel_north, modes
+        )
         projection = pl.pallas_call(
             functools.partial(kernel, nx, ny),
             out_shape=jax.ShapeDtypeStruct((MODES // ny, C), F32),
@@ -487,13 +490,10 @@
                 dma,
             ],
             compiler_params=pltpu.CompilerParams(
-                collective_id=0, has_side_effects=True
+                collective_id=0, has_side_effects=True, vmem_limit_bytes=40 << 20
             ),
             name="gradient",
-        )(
-            adj.reshape(C, WX, WY), field_mixing, time_mixing,
-            kernel_east, kernel_north, modes,
-        )
+        )(*[pltpu.with_memory_space_constraint(a, pltpu.HBM) for a in operands])
         return coefficients + projection
 
     in_specs = (P(None, None, "gx", "gy"), P(), P(), P(), P(), P("gx", "gy", None), P("gy", None))

time: 43.8 us -> 42.4 us (0.968)
  other arithmetic: 1.3 us -> 0.6 us
  Pallas kernels: 42.2 us -> 41.6 us
    add x1, other arithmetic: 1.3 us -> 0.6 us  [local(): return coefficients + projection]
    pallas_call x1, Pallas kernels: 42.2 us -> 41.6 us  [local(): pl.pallas_call(functools.partial(kernel, nx, ny), out_shape=jax.ShapeDtyp...]
where the time goes in v3:
time: 42.4 us; the launch traced here: 42.2 us
  Pallas kernels  41.6 us (98%)
  other arithmetic  0.6 us (1%)
    pallas_call x1, Pallas kernels, local(): pl.pallas_call(functools.partial(kernel, nx, ny), out_shape=jax.ShapeDtyp...  41.6 us

profile of v3, /device:TPU:1, one launch (start us, length us, event | category | flops | bytes accessed | tf_op | source)
XLA Modules:
  0.0 42.2 jit_solution(13711694227053828787)
XLA Ops:
  0.0 0.0 copy-start
  0.0 41.6 %gradient.1 = f32[16,24]{1,0:T(8,128)S(1)} custom-call(f32[24,32,256]{2,1,0:T(8,128)} %bitcast.1, f32[4,4]{1,0:T(4,128)} %fm_hbm.1, f32[6,6]{1,0:T(8,128)} %tm_hbm.1, f32[21]{0:T(128)} %ke_hbm.1, f32[21]{0:T(128)} %kn_hbm.1, bf16[32,256,256]{2,1,0:T(8,128)(2,1)} %modes_hbm.1), custom_call_target="tpu_custom_call" | custom-call | tf_op jit(solution)/shard_map/gradient/pallas_call | solution.py:450
  41.6 0.0 copy-done
  41.6 0.6 %add.3 = f32[16,24]{1,0:T(8,128)} add(f32[16,24]{1,0:T(8,128)S(1)} %copy-done, f32[16,24]{1,0:T(8,128)S(1)} %gradient.1) | non-fusion elementwise | flops 384 | bytes 4608 | tf_op jit(solution)/shard_map/add | solution.py:497
Async XLA Ops:
  0.0 41.6 %copy-start = (f32[16,24]{1,0:T(8,128)S(1)}, f32[16,24]{1,0:T(8,128)}, u32[]{:S(2)}) copy-start(f32[16,24]{1,0:T(8,128)} %param.13) | copy-start | bytes 4612

commit v4 on v3

--- a/solution.py
+++ b/solution.py
@@ -18,7 +18,7 @@
 SLAB = 384
 ROW = C
 NEAR = 4
-CHUNKS = ((0, NEAR), (4, 3), (7, 3))
+CHUNKS = ((0, NEAR), (4, 4), (8, 2))
 
 
 def dot(a, b):
@@ -80,9 +80,9 @@
         for i in range(2)
         for j in range(2)
     ]
-    for d in range(1, nx):
+    for d in sorted(range(1, nx), key=lambda d: -min(d // 2, nx // 2 - d // 2)):
         greet({"gx": gx ^ d})
-    for d in range(1, ny):
+    for d in sorted(range(1, ny), key=lambda d: -2 * (d & 12).bit_count() - (d & 3).bit_count()):
         greet({"gy": gy ^ d})
     greeted = nx + ny - 2
     for i, there, device in diagonal:

time: 42.4 us -> 42 us (level)
  no operation moved by 1% of the time
where the time goes in v4:
time: 42 us; the launch traced here: 41.9 us
  Pallas kernels  41.3 us (98%)
  other arithmetic  0.6 us (1%)
    pallas_call x1, Pallas kernels, local(): pl.pallas_call(functools.partial(kernel, nx, ny), out_shape=jax.ShapeDtyp...  41.3 us

profile of v4, /device:TPU:1, one launch (start us, length us, event | category | flops | bytes accessed | tf_op | source)
XLA Modules:
  0.0 41.9 jit_solution(11659526184046213838)
XLA Ops:
  0.0 0.0 copy-start
  0.0 41.3 %gradient.1 = f32[16,24]{1,0:T(8,128)S(1)} custom-call(f32[24,32,256]{2,1,0:T(8,128)} %bitcast.1, f32[4,4]{1,0:T(4,128)} %fm_hbm.1, f32[6,6]{1,0:T(8,128)} %tm_hbm.1, f32[21]{0:T(128)} %ke_hbm.1, f32[21]{0:T(128)} %kn_hbm.1, bf16[32,256,256]{2,1,0:T(8,128)(2,1)} %modes_hbm.1), custom_call_target="tpu_custom_call" | custom-call | tf_op jit(solution)/shard_map/gradient/pallas_call | solution.py:450
  41.3 0.0 copy-done
  41.3 0.6 %add.3 = f32[16,24]{1,0:T(8,128)} add(f32[16,24]{1,0:T(8,128)S(1)} %copy-done, f32[16,24]{1,0:T(8,128)S(1)} %gradient.1) | non-fusion elementwise | flops 384 | bytes 4608 | tf_op jit(solution)/shard_map/add | solution.py:497
Async XLA Ops:
  0.0 41.3 %copy-start = (f32[16,24]{1,0:T(8,128)S(1)}, f32[16,24]{1,0:T(8,128)}, u32[]{:S(2)}) copy-start(f32[16,24]{1,0:T(8,128)} %param.13) | copy-start | bytes 4612
